TPU v7x, 512 devices: a whole 4x8x8 slice. The times are simulated.
512 devices in a mesh: gx: 32 (over z_hi, y, core), gz: 16 (over z_lo, x).
Axes of the slice: x: 4, y: 8, z: 8 (z_hi: 2, z_lo: 4; z = z_hi * 4 + z_lo), core: 2. Of those that a mesh axis runs over, the one named last changes fastest.
Arguments:
- velocity: float32 [3, 2, 6144, 4096], P(None, None, 'gz', 'gx'), may hold values from -6 to 6
- metric_index: int32 [4096], P('gx'), may hold values from 0 to 63
- jac_table: float32 [64], replicated, may hold values from 0.5 to 2
- bend_table: float32 [64], replicated, may hold values from -1 to 1
Outputs:
- first_derivative: float32 [3, 2, 6144, 4096], P(None, None, 'gz', 'gx')
- second_derivative: float32 [3, 2, 6144, 4096], P(None, None, 'gz', 'gx')
- plane_energy: float32 [3, 2], replicated
Inputs may be any that keep to these rules, and one draw needn't show every extreme that they name: `metric_index`: each entry names a row of the metric tables.
All inputs are finite; a program needn't handle non-finite values.
Results may differ from a plain program's by a relative error of at most 0.00007.
Values sent between devices are 32-bit elements; how exact they have to be, the bound alone decides.
A program may use at most 64 MiB of HBM per device.

v0:
```python
import math

import jax
import jax.numpy as jnp
from jax import lax
from jax.sharding import PartitionSpec as P

alpha_one = 1.0 / 3.0
alpha_two = 2.0 / 11.0
reach = 24
highest = lax.Precision.HIGHEST


def band_matrix(rows, alpha):
    root = math.sqrt(1.0 - 4.0 * alpha * alpha)
    ratio = (1.0 - root) / (2.0 * alpha)
    factor = ratio / alpha / (1.0 - ratio * ratio)
    row_ids = jnp.arange(rows, dtype=jnp.int32)[:, None]
    col_ids = jnp.arange(rows + 2 * reach, dtype=jnp.int32)[None, :]
    offset = jnp.abs(col_ids - reach - row_ids)
    parity = jnp.where(offset % 2 == 0, 1.0, -1.0)
    power = jnp.exp(offset.astype(jnp.float32) * math.log(ratio))
    return jnp.where(offset <= reach, factor * parity * power, 0.0)


def stencil_matrix(rows, weights):
    row_ids = jnp.arange(rows, dtype=jnp.int32)[:, None]
    col_ids = jnp.arange(rows + 4, dtype=jnp.int32)[None, :]
    shift_ids = col_ids - row_ids - 2
    total = jnp.zeros((rows, rows + 4), jnp.float32)
    for shift_k, weight in zip((-2, -1, 0, 1, 2), weights):
        total = total + jnp.where(shift_ids == shift_k, weight, 0.0)
    return total


def line_operator(alpha, weights):
    block = 128
    band = band_matrix(block, alpha)
    stencil = stencil_matrix(block + 2 * reach, weights)
    joined = jnp.dot(band, stencil, precision=highest)
    start = block - reach - 2
    return jnp.pad(joined, ((0, 0), (start, 3 * block - start - joined.shape[1])))


def periodic_lines(columns):
    block = 128
    length = columns.shape[-1]
    lead = columns.shape[:-1]
    main = columns.reshape(lead + (length // block, block))
    before = jnp.roll(main, 1, axis=-2)
    after = jnp.roll(main, -1, axis=-2)
    weights_one = (-1.0 / 36.0, -7.0 / 9.0, 0.0, 7.0 / 9.0, 1.0 / 36.0)
    weights_two = (3.0 / 44.0, 12.0 / 11.0, -102.0 / 44.0, 12.0 / 11.0, 3.0 / 44.0)
    results = []
    for alpha, weights in ((alpha_one, weights_one), (alpha_two, weights_two)):
        whole_op = line_operator(alpha, weights)
        part = jnp.einsum("abcnm,im->abcni", before, whole_op[:, :block], precision=highest)
        part = part + jnp.einsum(
            "abcnm,im->abcni", main, whole_op[:, block : 2 * block], precision=highest
        )
        part = part + jnp.einsum(
            "abcnm,im->abcni", after, whole_op[:, 2 * block :], precision=highest
        )
        results.append(part.reshape(lead + (length,)))
    return (results[0], results[1])


def on_device(velocity, metric_index, jac_table, bend_table):
    first_line, second_line = periodic_lines(
        lax.all_to_all(velocity, "gx", split_axis=2, concat_axis=3, tiled=True)
    )
    first_xi = lax.all_to_all(first_line, "gx", split_axis=3, concat_axis=2, tiled=True)
    second_xi = lax.all_to_all(second_line, "gx", split_axis=3, concat_axis=2, tiled=True)
    table_rows = jac_table.shape[0]
    onehot = (metric_index[:, None] == jnp.arange(table_rows, dtype=jnp.int32)[None, :]).astype(
        jnp.float32
    )
    jac = jnp.dot(onehot, jac_table, precision=highest)
    bend = jnp.dot(onehot, bend_table, precision=highest)
    first = first_xi / jac
    second = (second_xi - bend * first) / (jac * jac)
    total_points = (
        metric_index.shape[0] * lax.axis_size("gx") * velocity.shape[2] * lax.axis_size("gz")
    )
    sums = lax.psum(jnp.sum(first * first, axis=(2, 3)), ("gx", "gz"))
    return (first, second, sums / total_points)


def solution(mesh):
    in_specs = (P(None, None, "gz", "gx"), P("gx"), P(), P())
    out_specs = (P(None, None, "gz", "gx"), P(None, None, "gz", "gx"), P())
    return jax.shard_map(
        on_device, mesh=mesh, in_specs=in_specs, out_specs=out_specs, check_vma=False
    )
```

profile of v0, /device:TPU:1, one launch (start us, length us, event | category | flops | bytes accessed | tf_op | source)
XLA Modules:
  0.0 331.4 jit_solution(7821478155496641981)
XLA Ops:
  0.6 3.2 copy.49
  3.9 17.2 %all-to-all-start = ((f32[3,2,384,128]{3,0,1,2:T(4,128)}), f32[3,2,384,128]{3,0,1,2:T(4,128)S(1)}, u32[]{:S(2)}, u32[]{:S(2)}) async-start(f32[3,2,384,128]{3,0,1,2:T(4,128)} %copy.49), calls=%async_computation | async-start | bytes 3145728 | tf_op jit(solution)/shard_map/all_to_all | solution.py:70
  21.1 1.1 fusion.18
  22.2 41.3 %all-to-all-done = f32[3,2,384,128]{3,0,1,2:T(4,128)S(1)} async-done(((f32[3,2,384,128]{3,0,1,2:T(4,128)}), f32[3,2,384,128]{3,0,1,2:T(4,128)S(1)}, u32[]{:S(2)}, u32[]{:S(2)}) %all-to-all-start) | async-done | bytes 1179680 | tf_op jit(solution)/shard_map/all_to_all | solution.py:70
  65.2 1.1 fusion.7
  67.4 2.2 fusion.1
  69.6 11.0 %copy.89 = f32[3,2,12,32,128]{2,1,0,4,3:T(2,128)} copy(f32[3,2,12,32,128]{4,3,2,1,0:T(8,128)} %fusion.1) | data formatting | bytes 2359296 | tf_op jit(solution)/shard_map/reshape | solution.py:64
  80.6 19.5 %reshape.37 = f32[32,1,9216]{2,1,0:T(1,128)} reshape(f32[4096,3,2,12]{3,2,1,0:T(2,128)} %bitcast.61) | data formatting | bytes 2359296
  100.1 6.5 %all-to-all-start.1 = ((f32[32,1,9216]{2,1,0:T(1,128)}), f32[32,1,9216]{2,1,0:T(1,128)}, u32[]{:S(2)}, u32[]{:S(2)}) async-start(f32[32,1,9216]{2,1,0:T(1,128)} %reshape.37), calls=%async_computation.1 | async-start | bytes 2359296 | tf_op jit(solution)/shard_map/all_to_all | solution.py:72
  107.4 1.1 fusion.6
  108.5 1.1 fusion.4
  109.6 1.1 fusion.3
  110.7 9.0 %copy.90 = f32[3,2,12,32,128]{2,1,0,4,3:T(2,128)} copy(f32[3,2,12,32,128]{4,3,2,1,0:T(8,128)S(1)} %fusion.3) | data formatting | bytes 2359296 | tf_op jit(solution)/shard_map/reshape | solution.py:64
  119.8 19.5 %reshape.39 = f32[32,1,9216]{2,1,0:T(1,128)} reshape(f32[4096,3,2,12]{3,2,1,0:T(2,128)} %bitcast.62) | data formatting | bytes 2359296
  140.0 11.7 %all-to-all-start.2 = ((f32[32,1,9216]{2,1,0:T(1,128)}), f32[32,1,9216]{2,1,0:T(1,128)S(1)}, u32[]{:S(2)}, u32[]{:S(2)}) async-start(f32[32,1,9216]{2,1,0:T(1,128)} %reshape.39), calls=%async_computation.2 | async-start | bytes 2359296 | tf_op jit(solution)/shard_map/all_to_all | solution.py:73
  152.4 4.8 %reduce.2 = f32[32,9216]{1,0:T(8,128)S(1)} reduce(f32[32,1,9216]{2,1,0:T(1,128)} %all-to-all-done.1, f32[]{:T(128)} %broadcast.111), dimensions={1}, to_apply=%all_to_all.40.reduce_sub_computation | reduce | bytes 2359300 | tf_op jit(solution)/shard_map/all_to_all | solution.py:72
  157.2 21.8 %reshape.38 = f32[4096,3,2,12]{3,2,1,0:T(2,128)} reshape(f32[32,9216]{1,0:T(8,128)S(1)} %reduce.2) | data formatting | bytes 2359296
  179.1 10.2 %copy.82 = f32[3,2,12,32,128]{4,3,1,2,0:T(8,128)S(1)} copy(f32[3,2,12,32,128]{2,1,0,4,3:T(2,128)} %bitcast.63) | data formatting | bytes 2359296 | tf_op jit(solution)/shard_map/all_to_all | solution.py:72
  190.1 100.3 %psum.7 = f32[3,2]{1,0:T(4,128)S(1)} all-reduce(f32[3,2]{1,0:T(4,128)S(1)} %multiply_reduce_fusion), channel_id=1, replica_groups=mesh['gx'=32,'gz'=16] {'gx','gz'}, use_global_device_ids=true, to_apply=%region_1.2 | all-reduce | flops 6 | bytes 48 | tf_op jit(solution)/shard_map/psum | solution.py:85
  291.9 3.5 %reduce.1 = f32[32,9216]{1,0:T(8,128)S(1)} reduce(f32[32,1,9216]{2,1,0:T(1,128)S(1)} %all-to-all-done.2, f32[]{:T(128)} %broadcast.111), dimensions={1}, to_apply=%all_to_all.44.reduce_sub_computation | reduce | bytes 2359300 | tf_op jit(solution)/shard_map/all_to_all | solution.py:73
  295.5 21.8 %reshape.40 = f32[4096,3,2,12]{3,2,1,0:T(2,128)} reshape(f32[32,9216]{1,0:T(8,128)S(1)} %reduce.1) | data formatting | bytes 2359296
  317.3 10.2 %copy.88 = f32[3,2,12,32,128]{4,3,1,2,0:T(8,128)S(1)} copy(f32[3,2,12,32,128]{2,1,0,4,3:T(2,128)} %bitcast.64) | data formatting | bytes 2359296 | tf_op jit(solution)/shard_map/all_to_all | solution.py:73
  329.2 1.1 copy.67
  330.3 1.1 copy.66
  (35 shorter events, 9.1 us)
Async XLA Ops:
  0.6 151.0 %copy-start = (f32[64]{0:T(128)S(1)}, f32[64]{0:T(128)}, u32[]{:S(2)}) copy-start(f32[64]{0:T(128)} %param.6) | copy-start | bytes 772
  3.9 59.7 %all-to-all-start = ((f32[3,2,384,128]{3,0,1,2:T(4,128)}), f32[3,2,384,128]{3,0,1,2:T(4,128)S(1)}, u32[]{:S(2)}, u32[]{:S(2)}) async-start(f32[3,2,384,128]{3,0,1,2:T(4,128)} %copy.49), calls=%async_computation | async-start | bytes 3145728 | tf_op jit(solution)/shard_map/all_to_all | solution.py:70
  64.3 0.6 copy-start.5
  64.3 2.0 copy-start.3
  64.3 0.9 copy-start.2
  100.1 39.8 %all-to-all-start.1 = ((f32[32,1,9216]{2,1,0:T(1,128)}), f32[32,1,9216]{2,1,0:T(1,128)}, u32[]{:S(2)}, u32[]{:S(2)}) async-start(f32[32,1,9216]{2,1,0:T(1,128)} %reshape.37), calls=%async_computation.1 | async-start | bytes 2359296 | tf_op jit(solution)/shard_map/all_to_all | solution.py:72
  106.6 0.8 copy-start.6
  107.4 1.1 copy-start.4
  139.3 12.4 %copy-start.7 = (s32[128]{0:T(128)S(1)}, s32[128]{0:T(128)}, u32[]{:S(2)}) copy-start(s32[128]{0:T(128)} %param.5) | copy-start | bytes 1540
  140.0 152.0 %all-to-all-start.2 = ((f32[32,1,9216]{2,1,0:T(1,128)}), f32[32,1,9216]{2,1,0:T(1,128)S(1)}, u32[]{:S(2)}, u32[]{:S(2)}) async-start(f32[32,1,9216]{2,1,0:T(1,128)} %reshape.39), calls=%async_computation.2 | async-start | bytes 2359296 | tf_op jit(solution)/shard_map/all_to_all | solution.py:73
  189.2 0.7 copy-start.8
  330.3 1.1 copy-start.1
where the time goes:
time: 333 us; the launch traced here: 331 us
  local copies, waits for them, and re-layouts  134 us (40%)
  blocking collectives  100 us (30%)
  waiting for transfers between devices  42 us (13%)
  starting transfers between devices  35.3 us (11%)
  matrix products  9.68 us (3%)
  other arithmetic  9.4 us (3%)
    psum x1, blocking collectives, on_device(): sums = lax.psum(jnp.sum(first * first, axis=(2, 3)), ('gx', 'gz'))  100 us
    unnamed x26, local copies, waits for them, and re-layouts  90.1 us
    all_to_all x1, waiting for transfers between devices, on_device(): lax.all_to_all(velocity, 'gx', split_axis=2, concat_axis=3, tiled=True)  41.3 us
    reshape x2, local copies, waits for them, and re-layouts, periodic_lines(): results.append(part.reshape(lead + (length,)))  20 us
    all_to_all x1, starting transfers between devices, on_device(): lax.all_to_all(velocity, 'gx', split_axis=2, concat_axis=3, tiled=True)  17.2 us
    all_to_all x1, starting transfers between devices, on_device(): lax.all_to_all(second_line, 'gx', split_axis=3, concat_axis=2, tiled=True)  11.7 us
    all_to_all x3, local copies, waits for them, and re-layouts, on_device(): lax.all_to_all(second_line, 'gx', split_axis=3, concat_axis=2, tiled=True)  11.6 us
    all_to_all x2, local copies, waits for them, and re-layouts, on_device(): lax.all_to_all(first_line, 'gx', split_axis=3, concat_axis=2, tiled=True)  11.1 us
  transfers between devices with their start and end apart: 3, of which 2 were waited for; matrix products, arithmetic and copies ran while one was open for 22% of the time, Pallas kernels for 0%

commit v1 on v0

v1 whole, which is shorter than its diff:
```python
import functools

import jax
import jax.numpy as jnp
import numpy as np
from jax import lax
from jax.experimental import pallas as pl
from jax.experimental.pallas import tpu as pltpu
from jax.sharding import PartitionSpec as P


MESH = pl.DeviceIdType.MESH
LANES = 128
WEIGHTS = (
    (1.0 / 3.0, (-1.0 / 36.0, -7.0 / 9.0, 0.0, 7.0 / 9.0, 1.0 / 36.0)),
    (2.0 / 11.0, (3.0 / 44.0, 12.0 / 11.0, -102.0 / 44.0, 12.0 / 11.0, 3.0 / 44.0)),
)


def constants():
    point = np.arange(LANES, dtype=np.float64)
    own, arrived = [], []
    leave = np.zeros((8, LANES))
    for which, (alpha, weights) in enumerate(WEIGHTS):
        ratio = (1.0 - np.sqrt(1.0 - 4.0 * alpha * alpha)) / (2.0 * alpha)
        factor = ratio / alpha / (1.0 - ratio * ratio)
        green = lambda d: factor * (-ratio) ** np.abs(d)
        kernel = lambda d: sum(w * green(d + k) for k, w in zip((-2, -1, 0, 1, 2), weights))
        own.append(kernel(point[None, :] - point[:, None]))
        rows = np.zeros((8, LANES))
        for side, sign in ((0, 1.0), (4, -1.0)):
            tail = kernel(sign * 2.0) / ratio**2
            away = point if side == 0 else LANES - 1 - point
            rows[side + which] = tail * (-ratio) ** (away + 1)
            rows[side + 2] = np.where(away == 0, kernel(sign) + tail * ratio, 0.0)
        arrived.append(rows)
        leave[which] = (-ratio) ** (LANES - 1 - point)
        leave[4 + which] = (-ratio) ** point
    leave[2, LANES - 1] = 1.0
    leave[6, 0] = 1.0
    return np.concatenate(own + arrived + [leave]).astype(np.float32)


def halves(array):
    high = array.astype(jnp.bfloat16)
    low = (array - high.astype(jnp.float32)).astype(jnp.bfloat16)
    return high, low


def kernel(
    places, groups, rows, points,
    x_hbm, const_hbm, index_hbm, jac_hbm, bend_hbm,
    first_hbm, second_hbm, energy_ref,
    x, const, index, jac_tab, bend_tab, split, first, second, op, edge_op,
    to_right, to_left, from_left, from_right, mine_a, slots_a, mine_b, slots_b,
    x_sem, in_sem, halo_send, halo_recv, a_send, a_recv, b_send, b_recv, out_sem,
):
    n_zh, n_y, n_core, n_zl, n_x = places
    n_gx = n_zh * n_y * n_core
    n_a, n_b = n_y * n_x, n_zh * n_zl * n_core
    gx, gz = lax.axis_index("gx"), lax.axis_index("gz")
    core = gx % n_core
    y = (gx // n_core) % n_y
    zh = gx // (n_core * n_y)
    xx = gz % n_x
    zl = gz // n_x
    in_a = y * n_x + xx
    in_b = (zh * n_zl + zl) * n_core + core

    def device_a(k):
        other = (in_a + k) % n_a
        return {"gx": (zh * n_y + other // n_x) * n_core + core, "gz": zl * n_x + other % n_x}

    def device_b(k):
        other = (in_b + k) % n_b
        other_z = other // n_core
        return {
            "gx": ((other_z // n_zl) * n_y + y) * n_core + other % n_core,
            "gz": (other_z % n_zl) * n_x + xx,
        }

    right = {"gx": (gx + 1) % n_gx, "gz": gz}
    left = {"gx": (gx + n_gx - 1) % n_gx, "gz": gz}

    def chunk(g):
        return pl.ds(pl.multiple_of(g * rows, rows), rows)

    def load(g):
        return pltpu.make_async_copy(x_hbm.at[chunk(g)], x.at[chunk(g)], x_sem.at[g])

    smalls = [
        pltpu.make_async_copy(src, dst, in_sem.at[n])
        for n, (src, dst) in enumerate(
            ((const_hbm, const), (index_hbm, index), (jac_hbm, jac_tab), (bend_hbm, bend_tab))
        )
    ]
    barrier = pltpu.get_barrier_semaphore()
    pl.semaphore_signal(barrier, inc=1, device_id=right, device_id_type=MESH)
    pl.semaphore_signal(barrier, inc=1, device_id=left, device_id_type=MESH)
    smalls[0].start()
    for g in range(groups):
        load(g).start()
    for copy in smalls[1:]:
        copy.start()

    @pl.loop(1, n_a)
    def _(k):
        pl.semaphore_signal(barrier, inc=1, device_id=device_a(k), device_id_type=MESH)

    @pl.loop(1, n_b)
    def _(k):
        pl.semaphore_signal(barrier, inc=1, device_id=device_b(k), device_id_type=MESH)

    smalls[0].wait()
    leave_high, leave_low = halves(const[272:280, :])
    leave = jnp.concatenate(
        [
            jnp.concatenate([leave_high, leave_high], axis=1),
            jnp.concatenate([leave_low, leave_low], axis=1),
        ],
        axis=0,
    )

    @pl.loop(0, groups)
    def _(g):
        load(g).wait()
        high, low = halves(x[chunk(g), :])
        both = jnp.concatenate([high, low], axis=1)
        split[chunk(g), :] = both
        sums = lax.dot_general(
            leave, both, (((1,), (1,)), ((), ())), preferred_element_type=jnp.float32
        )
        sums = sums[0:8] + sums[8:16]
        to_right[:, chunk(g)] = sums[0:4]
        to_left[:, chunk(g)] = sums[4:8]

    pl.semaphore_wait(barrier, 2 + (n_a - 1) + (n_b - 1))
    halo_r = pltpu.make_async_remote_copy(
        to_right, from_left, halo_send.at[0], halo_recv.at[0], device_id=right, device_id_type=MESH
    )
    halo_l = pltpu.make_async_remote_copy(
        to_left, from_right, halo_send.at[1], halo_recv.at[1], device_id=left, device_id_type=MESH
    )
    halo_r.start()
    halo_l.start()

    for copy in smalls[1:]:
        copy.wait()
    table_rows = jac_tab.shape[1]
    onehot = (
        lax.broadcasted_iota(jnp.int32, (table_rows, LANES), 0) == index[...]
    ).astype(jnp.float32)
    tables = jnp.concatenate(
        [jnp.broadcast_to(jac_tab[...], (8, table_rows)), jnp.broadcast_to(bend_tab[...], (8, table_rows))],
        axis=0,
    )
    metric = jnp.dot(tables, onehot, precision=lax.Precision.HIGHEST)
    inv_jac = 1.0 / metric[0:1]
    bend = metric[8:9]

    def scaled(one, two):
        one = one * inv_jac
        return jnp.concatenate([one, (two - bend * one) * (inv_jac * inv_jac)], axis=1)

    op_high, op_low = halves(scaled(const[0:128, :], const[128:256, :]))
    op[0:128, :] = op_high
    op[128:256, :] = op_low
    edge_high, edge_low = halves(scaled(const[256:264, :], const[264:272, :]))
    edge_op[...] = jnp.concatenate([edge_high, edge_high, edge_low, edge_low], axis=0)

    @pl.loop(0, groups)
    def _(g):
        both = split[chunk(g), :]
        high = op[0:128, :]
        low = op[128:256, :]
        part = jnp.dot(
            both, jnp.concatenate([high, high], axis=0), preferred_element_type=jnp.float32
        ) + jnp.dot(both, jnp.concatenate([low, low], axis=0), preferred_element_type=jnp.float32)
        first[chunk(g), :] = part[:, :LANES]
        second[chunk(g), :] = part[:, LANES:]

    halo_r.wait()
    halo_l.wait()
    lane = lax.broadcasted_iota(jnp.int32, (1, LANES), 1)

    def finish(g, energy):
        edge = jnp.concatenate([from_left[:, chunk(g)], from_right[:, chunk(g)]], axis=0)
        high = edge.astype(jnp.bfloat16).astype(jnp.float32)
        low = edge - high
        edge = jnp.concatenate([high, low, high, low], axis=0).T.astype(jnp.bfloat16)
        more = jnp.dot(edge, edge_op[...], preferred_element_type=jnp.float32)
        one = first[chunk(g), :] + more[:, :LANES]
        first[chunk(g), :] = one
        second[chunk(g), :] = second[chunk(g), :] + more[:, LANES:]
        square = jnp.sum(one * one, axis=0, keepdims=True)
        return energy + jnp.where(lane == g, jnp.sum(square, axis=1, keepdims=True), 0.0)

    energy = lax.fori_loop(0, groups, finish, jnp.zeros((1, LANES), jnp.float32))

    outs = [
        pltpu.make_async_copy(first, first_hbm, out_sem.at[0]),
        pltpu.make_async_copy(second, second_hbm, out_sem.at[1]),
    ]

    def send(n, here, mine, slots, device, send_sem, recv_sem):
        @pl.loop(1, n)
        def _(k):
            pltpu.make_async_remote_copy(
                mine, slots.at[here], send_sem, recv_sem, device_id=device(k), device_id_type=MESH
            ).start()

    def collect(n, slots, send_sem, recv_sem):
        rest = slots.at[pl.ds(0, n - 1)]
        pltpu.make_async_copy(rest, rest, recv_sem).wait()
        pltpu.make_async_copy(rest, rest, send_sem).wait()

    mine_a[...] = energy
    slots_a[in_a] = energy
    send(n_a, in_a, mine_a, slots_a, device_a, a_send, a_recv)
    for copy in outs:
        copy.start()
    collect(n_a, slots_a, a_send, a_recv)
    energy = jnp.sum(slots_a[...], axis=0)
    mine_b[...] = energy
    slots_b[in_b] = energy
    send(n_b, in_b, mine_b, slots_b, device_b, b_send, b_recv)
    collect(n_b, slots_b, b_send, b_recv)
    energy = jnp.sum(slots_b[...], axis=0) * (1.0 / points)
    width = energy_ref.shape[1]
    for row in range(energy_ref.shape[0]):
        energy_ref[row : row + 1, :] = energy[:, row * width : (row + 1) * width]
    for copy in outs:
        copy.wait()


def on_device(places, velocity, metric_index, jac_table, bend_table):
    n_zh, n_y, n_core, n_zl, n_x = places
    comps, planes, rows, lanes = velocity.shape
    groups = comps * planes
    lines = groups * rows
    table_rows = jac_table.shape[0]
    points = rows * n_zl * n_x * lanes * n_zh * n_y * n_core
    n_a, n_b = n_y * n_x, n_zh * n_zl * n_core
    f32, bf16 = jnp.float32, jnp.bfloat16
    const = jnp.asarray(constants())
    anywhere = pl.BlockSpec(memory_space=pl.ANY)
    dma = pltpu.SemaphoreType.DMA
    first, second, energy = pl.pallas_call(
        functools.partial(kernel, places, groups, rows, points),
        out_shape=(
            jax.ShapeDtypeStruct((lines, lanes), f32),
            jax.ShapeDtypeStruct((lines, lanes), f32),
            jax.ShapeDtypeStruct((comps, planes), f32),
        ),
        in_specs=[anywhere] * 5,
        out_specs=(anywhere, anywhere, pl.BlockSpec(memory_space=pltpu.VMEM)),
        scratch_shapes=[
            pltpu.VMEM((lines, lanes), f32),
            pltpu.VMEM(const.shape, f32),
            pltpu.VMEM((1, lanes), jnp.int32),
            pltpu.VMEM((1, table_rows), f32),
            pltpu.VMEM((1, table_rows), f32),
            pltpu.VMEM((lines, 2 * lanes), bf16),
            pltpu.VMEM((lines, lanes), f32),
            pltpu.VMEM((lines, lanes), f32),
            pltpu.VMEM((2 * lanes, 2 * lanes), bf16),
            pltpu.VMEM((32, 2 * lanes), bf16),
            pltpu.VMEM((4, lines), f32),
            pltpu.VMEM((4, lines), f32),
            pltpu.VMEM((4, lines), f32),
            pltpu.VMEM((4, lines), f32),
            pltpu.VMEM((1, lanes), f32),
            pltpu.VMEM((n_a, 1, lanes), f32),
            pltpu.VMEM((1, lanes), f32),
            pltpu.VMEM((n_b, 1, lanes), f32),
            dma((groups,)),
            dma((4,)),
            dma((2,)),
            dma((2,)),
            dma, dma, dma, dma,
            dma((2,)),
        ],
        compiler_params=pltpu.CompilerParams(collective_id=0, has_side_effects=True),
    )(
        velocity.reshape(lines, lanes),
        const,
        metric_index.reshape(1, lanes),
        jac_table.reshape(1, table_rows),
        bend_table.reshape(1, table_rows),
    )
    return (first.reshape(velocity.shape), second.reshape(velocity.shape), energy)


def solution(mesh):
    n_gx, n_gz = mesh.shape["gx"], mesh.shape["gz"]
    n_x = min(4, n_gz)
    places = (2, n_gx // 4, 2, n_gz // n_x, n_x)
    in_specs = (P(None, None, "gz", "gx"), P("gx"), P(), P())
    out_specs = (P(None, None, "gz", "gx"), P(None, None, "gz", "gx"), P())
    return jax.shard_map(
        functools.partial(on_device, places),
        mesh=mesh, in_specs=in_specs, out_specs=out_specs, check_vma=False,
    )
```

time: 333 us -> 38.1 us (0.11)
  local copies, waits for them, and re-layouts: 134 us -> 4.79 us
  blocking collectives: 100 us -> 0 us
  waiting for transfers between devices: 42 us -> 0 us
  starting transfers between devices: 35.3 us -> 0 us
  Pallas kernels: 0 us -> 32.5 us
  matrix products: 9.68 us -> 0 us
  other arithmetic: 9.4 us -> 0 us
    psum x1 -> x0, blocking collectives: 100 us -> none  [on_device(): sums = lax.psum(jnp.sum(first * first, axis=(2, 3)), ('gx', 'gz'))]
    unnamed x26 -> x5, local copies, waits for them, and re-layouts: 90.1 us -> 4.79 us
    all_to_all x3 -> x0, waiting for transfers between devices: 42 us -> none  [the longest x1 41.3 us: on_device(): lax.all_to_all(velocity, 'gx', split_axis=2, concat_axis=3, tiled=True)]
    all_to_all x3 -> x0, starting transfers between devices: 35.3 us -> none  [the longest x1 17.2 us: on_device(): lax.all_to_all(velocity, 'gx', split_axis=2, concat_axis=3, tiled=True)]
    pallas_call x0 -> x1, Pallas kernels: none -> 32.5 us  [on_device(): pl.pallas_call(functools.partial(kernel, places, groups, rows, points), o...]
    all_to_all x6 -> x0, local copies, waits for them, and re-layouts: 23.4 us -> none  [the longest x3 11.6 us: on_device(): lax.all_to_all(second_line, 'gx', split_axis=3, concat_axis=2, tiled=True)]
    reshape x2 -> x0, local copies, waits for them, and re-layouts: 20 us -> none  [periodic_lines(): results.append(part.reshape(lead + (length,)))]
    dot_general x10 -> x0, matrix products: 9.68 us -> none  [the longest x2 3.35 us: periodic_lines(): jnp.einsum('abcnm,im->abcni', main, whole_op[:, block:2 * block], precisi...]
  transfers between devices with their start and end apart: 3 -> 0, of which waited for: 2 -> 0; matrix products, arithmetic and copies ran while one was open for 22% -> 0% of each run, Pallas kernels for 0% -> 0%
where the time goes in v1:
time: 38.1 us; the launch traced here: 37.9 us
  Pallas kernels  32.5 us (85%)
  local copies, waits for them, and re-layouts  4.79 us (13%)
  between operations  0.64 us (2%)
    pallas_call x1, Pallas kernels, on_device(): pl.pallas_call(functools.partial(kernel, places, groups, rows, points), o...  32.5 us
    unnamed x5, local copies, waits for them, and re-layouts  4.79 us

profile of v1, /device:TPU:1, one launch (start us, length us, event | category | flops | bytes accessed | tf_op | source)
XLA Modules:
  0.0 37.9 jit_solution(10964963478476378483)
XLA Ops:
  0.6 32.5 %shard_map.76 = (f32[2304,128]{1,0:T(8,128)}, f32[2304,128]{1,0:T(8,128)}, f32[3,2]{1,0:T(4,128)}) custom-call(f32[2304,128]{1,0:T(8,128)} %bitcast.8, f32[280,128]{1,0:T(8,128)} %constant.2.clone.const_hbm, s32[1,128]{1,0:T(1,128)} %bitcast.9, f32[1,64]{1,0:T(1,128)} %bitcast.10, f32[1,64]{1,0:T(1,128)} %bitcast.11), custom_call_target="tpu_custom_call" | custom-call | tf_op jit(solution)/shard_map/pallas_call | solution.py:248
  33.2 1.3 %copy.8 = f32[3,2]{0,1:T(2,128)} copy(f32[3,2]{1,0:T(4,128)} %get-tuple-element.11) | data formatting | bytes 48
  34.5 0.0 copy-start
  34.5 2.5 %copy.11 = f32[3,2,384,128]{3,2,1,0:T(8,128)} copy(f32[3,2,384,128]{3,2,1,0:T(8,128)} %bitcast.7) | data formatting | bytes 2359296
  36.9 0.0 copy-done
  36.9 1.0 %copy.12 = f32[3,2,384,128]{3,2,1,0:T(8,128)} copy(f32[3,2,384,128]{3,2,1,0:T(8,128)S(1)} %bitcast.6) | data formatting | bytes 2359296
Async XLA Ops:
  34.5 2.5 %copy-start = (f32[2304,128]{1,0:T(8,128)S(1)}, f32[2304,128]{1,0:T(8,128)}, u32[]{:S(2)}) copy-start(f32[2304,128]{1,0:T(8,128)} %get-tuple-element.7) | copy-start | bytes 3538948

commit v2 on v1

--- a/solution.py
+++ b/solution.py
@@ -50,34 +50,47 @@
 def kernel(
     places, groups, rows, points,
     x_hbm, const_hbm, index_hbm, jac_hbm, bend_hbm,
-    first_hbm, second_hbm, energy_ref,
-    x, const, index, jac_tab, bend_tab, split, first, second, op, edge_op,
+    first, second, energy_ref,
+    x, const, index, jac_tab, bend_tab, split, edge_t, op, edge_op, squares,
     to_right, to_left, from_left, from_right, mine_a, slots_a, mine_b, slots_b,
-    x_sem, in_sem, halo_send, halo_recv, a_send, a_recv, b_send, b_recv, out_sem,
+    x_sem, in_sem, halo_send, halo_recv, a_send, a_recv, b_send, b_recv,
 ):
     n_zh, n_y, n_core, n_zl, n_x = places
     n_gx = n_zh * n_y * n_core
-    n_a, n_b = n_y * n_x, n_zh * n_zl * n_core
+    n_z = n_zh * n_zl
+    halves_x = n_x // 2
+    n_a, n_b = n_y * 2, n_z * n_core * halves_x
     gx, gz = lax.axis_index("gx"), lax.axis_index("gz")
     core = gx % n_core
     y = (gx // n_core) % n_y
     zh = gx // (n_core * n_y)
     xx = gz % n_x
     zl = gz // n_x
-    in_a = y * n_x + xx
-    in_b = (zh * n_zl + zl) * n_core + core
-
-    def device_a(k):
-        other = (in_a + k) % n_a
-        return {"gx": (zh * n_y + other // n_x) * n_core + core, "gz": zl * n_x + other % n_x}
-
-    def device_b(k):
-        other = (in_b + k) % n_b
-        other_z = other // n_core
-        return {
-            "gx": ((other_z // n_zl) * n_y + y) * n_core + other % n_core,
-            "gz": (other_z % n_zl) * n_x + xx,
-        }
+    z = zh * n_zl + zl
+    in_a = y * 2 + xx % 2
+    in_b = (z * n_core + core) * halves_x + xx // 2
+
+    def turned(place, by, size):
+        place = place + by
+        return jnp.where(place >= size, place - size, place)
+
+    pair_a = xx + 1 - 2 * (xx % 2)
+    ys = [(zh * n_y + turned(y, by, n_y)) * n_core + core for by in range(n_y)]
+    peers_a = [
+        (min(by, n_y - by) + across, ys[by], zl * n_x + (pair_a if across else xx))
+        for by in range(n_y) for across in range(2) if by + across
+    ]
+    zs = [turned(z, by, n_z) for by in range(n_z)]
+    peers_b = [
+        (
+            min(by, n_z - by) + across,
+            ((zs[by] // n_zl) * n_y + y) * n_core + (1 - core if other else core),
+            (zs[by] % n_zl) * n_x + (n_x - 1 - xx if across else xx),
+        )
+        for by in range(n_z) for other in range(n_core) for across in range(halves_x) if by + other + across
+    ]
+    peers_a = [{"gx": p[1], "gz": p[2]} for p in sorted(peers_a, key=lambda p: -p[0])]
+    peers_b = [{"gx": p[1], "gz": p[2]} for p in sorted(peers_b, key=lambda p: -p[0])]
 
     right = {"gx": (gx + 1) % n_gx, "gz": gz}
     left = {"gx": (gx + n_gx - 1) % n_gx, "gz": gz}
@@ -103,13 +116,8 @@
     for copy in smalls[1:]:
         copy.start()
 
-    @pl.loop(1, n_a)
-    def _(k):
-        pl.semaphore_signal(barrier, inc=1, device_id=device_a(k), device_id_type=MESH)
-
-    @pl.loop(1, n_b)
-    def _(k):
-        pl.semaphore_signal(barrier, inc=1, device_id=device_b(k), device_id_type=MESH)
+    for peer in peers_a + peers_b:
+        pl.semaphore_signal(barrier, inc=1, device_id=peer, device_id_type=MESH)
 
     smalls[0].wait()
     leave_high, leave_low = halves(const[272:280, :])
@@ -181,32 +189,25 @@
 
     halo_r.wait()
     halo_l.wait()
-    lane = lax.broadcasted_iota(jnp.int32, (1, LANES), 1)
-
-    def finish(g, energy):
+
+    squares[...] = jnp.zeros_like(squares)
+
+    @pl.loop(0, groups)
+    def _(g):
         edge = jnp.concatenate([from_left[:, chunk(g)], from_right[:, chunk(g)]], axis=0)
         high = edge.astype(jnp.bfloat16).astype(jnp.float32)
         low = edge - high
         edge = jnp.concatenate([high, low, high, low], axis=0).T.astype(jnp.bfloat16)
-        more = jnp.dot(edge, edge_op[...], preferred_element_type=jnp.float32)
-        one = first[chunk(g), :] + more[:, :LANES]
+        edge_t[chunk(g), :] = edge
+        more = jnp.dot(edge, edge_op[:, :LANES], preferred_element_type=jnp.float32)
+        one = first[chunk(g), :] + more
         first[chunk(g), :] = one
-        second[chunk(g), :] = second[chunk(g), :] + more[:, LANES:]
-        square = jnp.sum(one * one, axis=0, keepdims=True)
-        return energy + jnp.where(lane == g, jnp.sum(square, axis=1, keepdims=True), 0.0)
-
-    energy = lax.fori_loop(0, groups, finish, jnp.zeros((1, LANES), jnp.float32))
-
-    outs = [
-        pltpu.make_async_copy(first, first_hbm, out_sem.at[0]),
-        pltpu.make_async_copy(second, second_hbm, out_sem.at[1]),
-    ]
-
-    def send(n, here, mine, slots, device, send_sem, recv_sem):
-        @pl.loop(1, n)
-        def _(k):
+        squares[pl.ds(g, 1), :] = jnp.sum(one * one, axis=0, keepdims=True)
+
+    def send(here, mine, slots, peers, send_sem, recv_sem):
+        for peer in peers:
             pltpu.make_async_remote_copy(
-                mine, slots.at[here], send_sem, recv_sem, device_id=device(k), device_id_type=MESH
+                mine, slots.at[here], send_sem, recv_sem, device_id=peer, device_id_type=MESH
             ).start()
 
     def collect(n, slots, send_sem, recv_sem):
@@ -214,21 +215,42 @@
         pltpu.make_async_copy(rest, rest, recv_sem).wait()
         pltpu.make_async_copy(rest, rest, send_sem).wait()
 
+    diagonal = lax.broadcasted_iota(jnp.int32, (8, LANES), 0) == lax.broadcasted_iota(
+        jnp.int32, (8, LANES), 1
+    )
+    energy = jnp.sum(squares[...], axis=1, keepdims=True)
+    energy = jnp.sum(jnp.where(diagonal, energy, 0.0), axis=0, keepdims=True)
     mine_a[...] = energy
     slots_a[in_a] = energy
-    send(n_a, in_a, mine_a, slots_a, device_a, a_send, a_recv)
-    for copy in outs:
-        copy.start()
+    send(in_a, mine_a, slots_a, peers_a, a_send, a_recv)
+
+    @pl.loop(0, groups)
+    def _(g):
+        more = jnp.dot(edge_t[chunk(g), :], edge_op[:, LANES:], preferred_element_type=jnp.float32)
+        second[chunk(g), :] = second[chunk(g), :] + more
+
     collect(n_a, slots_a, a_send, a_recv)
     energy = jnp.sum(slots_a[...], axis=0)
     mine_b[...] = energy
     slots_b[in_b] = energy
-    send(n_b, in_b, mine_b, slots_b, device_b, b_send, b_recv)
+    send(in_b, mine_b, slots_b, peers_b, b_send, b_recv)
     collect(n_b, slots_b, b_send, b_recv)
-    energy = jnp.sum(slots_b[...], axis=0) * (1.0 / points)
-    width = energy_ref.shape[1]
-    for row in range(energy_ref.shape[0]):
-        energy_ref[row : row + 1, :] = energy[:, row * width : (row + 1) * width]
+    energy_ref[...] = jnp.sum(slots_b[...], axis=0) * (1.0 / points)
+
+
+def store(first, second, energy_ref, first_hbm, second_hbm, out_ref, sems):
+    outs = [
+        pltpu.make_async_copy(first, first_hbm, sems.at[0]),
+        pltpu.make_async_copy(second, second_hbm, sems.at[1]),
+    ]
+    for copy in outs:
+        copy.start()
+    planes, comps = out_ref.shape
+    energy = energy_ref[...]
+    for row in range(planes):
+        for col in range(comps):
+            at = col * planes + row
+            out_ref[row : row + 1, col : col + 1] = energy[:, at : at + 1]
     for copy in outs:
         copy.wait()
 
@@ -240,20 +262,21 @@
     lines = groups * rows
     table_rows = jac_table.shape[0]
     points = rows * n_zl * n_x * lanes * n_zh * n_y * n_core
-    n_a, n_b = n_y * n_x, n_zh * n_zl * n_core
+    n_a, n_b = n_y * 2, n_zh * n_zl * n_core * (n_x // 2)
     f32, bf16 = jnp.float32, jnp.bfloat16
     const = jnp.asarray(constants())
     anywhere = pl.BlockSpec(memory_space=pl.ANY)
+    vmem = pl.BlockSpec(memory_space=pltpu.VMEM)
     dma = pltpu.SemaphoreType.DMA
     first, second, energy = pl.pallas_call(
         functools.partial(kernel, places, groups, rows, points),
         out_shape=(
-            jax.ShapeDtypeStruct((lines, lanes), f32),
-            jax.ShapeDtypeStruct((lines, lanes), f32),
-            jax.ShapeDtypeStruct((comps, planes), f32),
+            pltpu.VMEM((lines, lanes), f32),
+            pltpu.VMEM((lines, lanes), f32),
+            pltpu.VMEM((1, lanes), f32),
         ),
         in_specs=[anywhere] * 5,
-        out_specs=(anywhere, anywhere, pl.BlockSpec(memory_space=pltpu.VMEM)),
+        out_specs=(vmem, vmem, vmem),
         scratch_shapes=[
             pltpu.VMEM((lines, lanes), f32),
             pltpu.VMEM(const.shape, f32),
@@ -261,10 +284,10 @@
             pltpu.VMEM((1, table_rows), f32),
             pltpu.VMEM((1, table_rows), f32),
             pltpu.VMEM((lines, 2 * lanes), bf16),
-            pltpu.VMEM((lines, lanes), f32),
-            pltpu.VMEM((lines, lanes), f32),
+            pltpu.VMEM((lines, 32), bf16),
             pltpu.VMEM((2 * lanes, 2 * lanes), bf16),
             pltpu.VMEM((32, 2 * lanes), bf16),
+            pltpu.VMEM((8, lanes), f32),
             pltpu.VMEM((4, lines), f32),
             pltpu.VMEM((4, lines), f32),
             pltpu.VMEM((4, lines), f32),
@@ -278,7 +301,6 @@
             dma((2,)),
             dma((2,)),
             dma, dma, dma, dma,
-            dma((2,)),
         ],
         compiler_params=pltpu.CompilerParams(collective_id=0, has_side_effects=True),
     )(
@@ -288,7 +310,15 @@
         jac_table.reshape(1, table_rows),
         bend_table.reshape(1, table_rows),
     )
-    return (first.reshape(velocity.shape), second.reshape(velocity.shape), energy)
+    whole = jax.ShapeDtypeStruct((lines, lanes), f32)
+    first, second, energy = pl.pallas_call(
+        store,
+        out_shape=(whole, whole, jax.ShapeDtypeStruct((planes, comps), f32)),
+        in_specs=[vmem] * 3,
+        out_specs=(anywhere, anywhere, vmem),
+        scratch_shapes=[dma((2,))],
+    )(*(pltpu.with_memory_space_constraint(a, pltpu.VMEM) for a in (first, second, energy)))
+    return (first.reshape(velocity.shape), second.reshape(velocity.shape), energy.T)
 
 
 def solution(mesh):

time: 38.1 us -> 33.5 us (0.88)
  local copies, waits for them, and re-layouts: 4.79 us -> 0 us
    unnamed x5 -> x0, local copies, waits for them, and re-layouts: 4.79 us -> none
    pallas_call x0 -> x1, Pallas kernels: none -> 1.98 us  [on_device(): pl.pallas_call(store, out_shape=(whole, whole, jax.ShapeDtypeStruct((plan...]
    pallas_call x1, Pallas kernels: 32.5 us -> 30.8 us  [on_device(): pl.pallas_call(functools.partial(kernel, places, groups, rows, points), o...]
where the time goes in v2:
time: 33.5 us; the launch traced here: 33.4 us
  Pallas kernels  32.8 us (98%)
  between operations  0.64 us (2%)
    pallas_call x1, Pallas kernels, on_device(): pl.pallas_call(functools.partial(kernel, places, groups, rows, points), o...  30.8 us
    pallas_call x1, Pallas kernels, on_device(): pl.pallas_call(store, out_shape=(whole, whole, jax.ShapeDtypeStruct((plan...  1.98 us

profile of v2, /device:TPU:1, one launch (start us, length us, event | category | flops | bytes accessed | tf_op | source)
XLA Modules:
  0.0 33.4 jit_solution(17373016662766252105)
XLA Ops:
  0.6 30.8 %shard_map.76 = (f32[2304,128]{1,0:T(8,128)S(1)}, f32[2304,128]{1,0:T(8,128)S(1)}, f32[1,128]{1,0:T(1,128)S(1)}) custom-call(f32[2304,128]{1,0:T(8,128)} %bitcast.7, f32[280,128]{1,0:T(8,128)} %constant.2.clone.const_hbm, s32[1,128]{1,0:T(1,128)} %bitcast.8, f32[1,64]{1,0:T(1,128)} %bitcast.9, f32[1,64]{1,0:T(1,128)} %bitcast.10), custom_call_target="tpu_custom_call" | custom-call | tf_op jit(solution)/shard_map/pallas_call | solution.py:271
  31.4 2.0 %shard_map.77 = (f32[2304,128]{1,0:T(8,128)}, f32[2304,128]{1,0:T(8,128)}, f32[2,3]{1,0:T(2,128)}) custom-call(f32[2304,128]{1,0:T(8,128)S(1)} %get-tuple-element.9.first, f32[2304,128]{1,0:T(8,128)S(1)} %get-tuple-element.10.second, f32[1,128]{1,0:T(1,128)S(1)} %get-tuple-element.11.energy_ref), custom_call_target="tpu_custom_call" | custom-call | tf_op jit(solution)/shard_map/pallas_call | solution.py:314

commit v3 on v2

--- a/solution.py
+++ b/solution.py
@@ -52,8 +52,9 @@
     x_hbm, const_hbm, index_hbm, jac_hbm, bend_hbm,
     first, second, energy_ref,
     x, const, index, jac_tab, bend_tab, split, edge_t, op, edge_op, squares,
-    to_right, to_left, from_left, from_right, mine_a, slots_a, mine_b, slots_b,
-    x_sem, in_sem, halo_send, halo_recv, a_send, a_recv, b_send, b_recv,
+    to_right, to_left, from_left, from_right, from_far, to_middle_r, to_middle_l, middle,
+    mine_a, slots_a, mine_b, slots_b,
+    x_sem, in_sem, halo_send, halo_recv, far_recv, mid_send, mid_recv, a_send, a_recv, b_send, b_recv,
 ):
     n_zh, n_y, n_core, n_zl, n_x = places
     n_gx = n_zh * n_y * n_core
@@ -92,6 +93,19 @@
     peers_a = [{"gx": p[1], "gz": p[2]} for p in sorted(peers_a, key=lambda p: -p[0])]
     peers_b = [{"gx": p[1], "gz": p[2]} for p in sorted(peers_b, key=lambda p: -p[0])]
 
+    lines = groups * rows
+    quarter = n_z // 4
+    is_last = jnp.logical_and(y == n_y - 1, core == n_core - 1)
+    is_first = jnp.logical_and(y == 0, core == 0)
+
+    def in_z(by, at_last):
+        there = turned(z, by % n_z, n_z)
+        within = n_y * n_core - 1 if at_last else 0
+        return {"gx": (there // n_zl) * n_y * n_core + within, "gz": (there % n_zl) * n_x + xx}
+
+    ahead, behind = in_z(quarter, True), in_z(-quarter, True)
+    ahead_first = in_z(quarter, False)
+
     right = {"gx": (gx + 1) % n_gx, "gz": gz}
     left = {"gx": (gx + n_gx - 1) % n_gx, "gz": gz}
 
@@ -110,17 +124,69 @@
     barrier = pltpu.get_barrier_semaphore()
     pl.semaphore_signal(barrier, inc=1, device_id=right, device_id_type=MESH)
     pl.semaphore_signal(barrier, inc=1, device_id=left, device_id_type=MESH)
-    smalls[0].start()
+    for copy in smalls:
+        copy.start()
     for g in range(groups):
         load(g).start()
-    for copy in smalls[1:]:
-        copy.start()
 
     for peer in peers_a + peers_b:
         pl.semaphore_signal(barrier, inc=1, device_id=peer, device_id_type=MESH)
 
-    smalls[0].wait()
-    leave_high, leave_low = halves(const[272:280, :])
+    @pl.when(is_last)
+    def _():
+        for peer in (ahead, behind, ahead_first):
+            pl.semaphore_signal(barrier, inc=1, device_id=peer, device_id_type=MESH)
+        from_right[...] = jnp.zeros_like(from_right)
+
+    @pl.when(is_first)
+    def _():
+        pl.semaphore_signal(barrier, inc=1, device_id=behind, device_id_type=MESH)
+        from_left[...] = jnp.zeros_like(from_left)
+
+    for copy in smalls:
+        copy.wait()
+    table_rows = jac_tab.shape[1]
+    onehot = (
+        lax.broadcasted_iota(jnp.int32, (table_rows, LANES), 0) == index[...]
+    ).astype(jnp.float32)
+    tables = jnp.concatenate(
+        [jnp.broadcast_to(jac_tab[...], (8, table_rows)), jnp.broadcast_to(bend_tab[...], (8, table_rows))],
+        axis=0,
+    )
+    metric = jnp.dot(tables, onehot, precision=lax.Precision.HIGHEST)
+    inv_jac = 1.0 / metric[0:1]
+    bend = metric[8:9]
+
+    def scaled(one, two):
+        one = one * inv_jac
+        return jnp.concatenate([one, (two - bend * one) * (inv_jac * inv_jac)], axis=1)
+
+    own_op = scaled(const[0:128, :], const[128:256, :])
+    arrived_op = scaled(const[256:264, :], const[264:272, :])
+    arrived_one = arrived_op[:, :LANES]
+    joint = lax.dot_general(
+        arrived_one, own_op[:, :LANES], (((1,), (1,)), ((), ())),
+        precision=lax.Precision.HIGHEST, preferred_element_type=jnp.float32,
+    )
+    for ref, at in ((to_middle_l, 0), (to_middle_r, 4)):
+        sums_of, edge_of = arrived_one[at : at + 1], arrived_one[at + 2 : at + 3]
+        for row, (product, times) in enumerate(
+            ((sums_of * sums_of, 1.0), (sums_of * edge_of, 2.0), (edge_of * edge_of, 1.0))
+        ):
+            total = jnp.sum(product, axis=1, keepdims=True) * times
+            ref[row : row + 1, lines:] = jnp.broadcast_to(total, (1, LANES))
+        ref[3:4, lines:] = jnp.zeros((1, LANES), jnp.float32)
+    out_rows = const[272:280, :]
+    leave_high, leave_low = halves(
+        jnp.concatenate(
+            [
+                out_rows,
+                out_rows[0:1], out_rows[2:3], joint[4:5], joint[6:7],
+                out_rows[4:5], out_rows[6:7], joint[0:1], joint[2:3],
+            ],
+            axis=0,
+        )
+    )
     leave = jnp.concatenate(
         [
             jnp.concatenate([leave_high, leave_high], axis=1),
@@ -138,42 +204,57 @@
         sums = lax.dot_general(
             leave, both, (((1,), (1,)), ((), ())), preferred_element_type=jnp.float32
         )
-        sums = sums[0:8] + sums[8:16]
+        sums = sums[0:16] + sums[16:32]
         to_right[:, chunk(g)] = sums[0:4]
         to_left[:, chunk(g)] = sums[4:8]
-
-    pl.semaphore_wait(barrier, 2 + (n_a - 1) + (n_b - 1))
+        to_middle_r[:, chunk(g)] = sums[8:12]
+        to_middle_l[:, chunk(g)] = sums[12:16]
+
+    pl.semaphore_wait(
+        barrier, 2 + (n_a - 1) + (n_b - 1) + jnp.where(is_last, 3, jnp.where(is_first, 1, 0))
+    )
+    middle_r = pltpu.make_async_remote_copy(
+        to_middle_r, middle.at[0], mid_send, mid_recv.at[0], device_id=ahead, device_id_type=MESH
+    )
+    middle_l = pltpu.make_async_remote_copy(
+        to_middle_l, middle.at[1], mid_send, mid_recv.at[1], device_id=behind, device_id_type=MESH
+    )
     halo_r = pltpu.make_async_remote_copy(
         to_right, from_left, halo_send.at[0], halo_recv.at[0], device_id=right, device_id_type=MESH
     )
     halo_l = pltpu.make_async_remote_copy(
         to_left, from_right, halo_send.at[1], halo_recv.at[1], device_id=left, device_id_type=MESH
     )
-    halo_r.start()
-    halo_l.start()
-
-    for copy in smalls[1:]:
-        copy.wait()
-    table_rows = jac_tab.shape[1]
-    onehot = (
-        lax.broadcasted_iota(jnp.int32, (table_rows, LANES), 0) == index[...]
-    ).astype(jnp.float32)
-    tables = jnp.concatenate(
-        [jnp.broadcast_to(jac_tab[...], (8, table_rows)), jnp.broadcast_to(bend_tab[...], (8, table_rows))],
-        axis=0,
-    )
-    metric = jnp.dot(tables, onehot, precision=lax.Precision.HIGHEST)
-    inv_jac = 1.0 / metric[0:1]
-    bend = metric[8:9]
-
-    def scaled(one, two):
-        one = one * inv_jac
-        return jnp.concatenate([one, (two - bend * one) * (inv_jac * inv_jac)], axis=1)
-
-    op_high, op_low = halves(scaled(const[0:128, :], const[128:256, :]))
+    far_r = pltpu.make_async_remote_copy(
+        to_right, from_far, halo_send.at[0], far_recv, device_id=right, device_id_type=MESH
+    )
+    far_l = pltpu.make_async_remote_copy(
+        to_left, from_far, halo_send.at[1], far_recv, device_id=left, device_id_type=MESH
+    )
+
+    @pl.when(is_last)
+    def _():
+        middle_r.start()
+        halo_l.start()
+        far_r.start()
+
+    @pl.when(is_first)
+    def _():
+        middle_l.start()
+        halo_r.start()
+        far_l.start()
+
+    is_inner = jnp.logical_not(jnp.logical_or(is_last, is_first))
+
+    @pl.when(is_inner)
+    def _():
+        halo_r.start()
+        halo_l.start()
+
+    op_high, op_low = halves(own_op)
     op[0:128, :] = op_high
     op[128:256, :] = op_low
-    edge_high, edge_low = halves(scaled(const[256:264, :], const[264:272, :]))
+    edge_high, edge_low = halves(arrived_op)
     edge_op[...] = jnp.concatenate([edge_high, edge_high, edge_low, edge_low], axis=0)
 
     @pl.loop(0, groups)
@@ -187,23 +268,54 @@
         first[chunk(g), :] = part[:, :LANES]
         second[chunk(g), :] = part[:, LANES:]
 
-    halo_r.wait()
-    halo_l.wait()
+    @pl.when(jnp.logical_not(is_first))
+    def _():
+        halo_r.wait_recv()
+
+    @pl.when(jnp.logical_not(is_last))
+    def _():
+        halo_l.wait_recv()
+
+    def spread(left_edge, right_edge):
+        edge = jnp.concatenate([left_edge, right_edge], axis=0)
+        high = edge.astype(jnp.bfloat16).astype(jnp.float32)
+        low = edge - high
+        return jnp.concatenate([high, low, high, low], axis=0).T.astype(jnp.bfloat16)
 
     squares[...] = jnp.zeros_like(squares)
 
     @pl.loop(0, groups)
     def _(g):
-        edge = jnp.concatenate([from_left[:, chunk(g)], from_right[:, chunk(g)]], axis=0)
-        high = edge.astype(jnp.bfloat16).astype(jnp.float32)
-        low = edge - high
-        edge = jnp.concatenate([high, low, high, low], axis=0).T.astype(jnp.bfloat16)
+        edge = spread(from_left[:, chunk(g)], from_right[:, chunk(g)])
         edge_t[chunk(g), :] = edge
         more = jnp.dot(edge, edge_op[:, :LANES], preferred_element_type=jnp.float32)
         one = first[chunk(g), :] + more
         first[chunk(g), :] = one
         squares[pl.ds(g, 1), :] = jnp.sum(one * one, axis=0, keepdims=True)
 
+    @pl.when(is_last)
+    def _():
+        middle_r.wait_recv()
+        middle_l.wait_recv()
+        whole = pl.ds(0, lines)
+        right_sum, right_edge = middle[0, 0:1, whole], middle[0, 1:2, whole]
+        left_sum, left_edge = middle[1, 0:1, whole], middle[1, 1:2, whole]
+
+        def again(side, row):
+            return jnp.concatenate([middle[side, row : row + 1, lines:]] * (lines // LANES), axis=1)
+
+        cross = 2.0 * (
+            right_sum * middle[1, 2:3, whole] + right_edge * middle[1, 3:4, whole]
+            + left_sum * middle[0, 2:3, whole] + left_edge * middle[0, 3:4, whole]
+        )
+        for side, some, edge in ((1, right_sum, right_edge), (0, left_sum, left_edge)):
+            cross += some * (again(side, 0) * some + again(side, 1) * edge) + again(side, 2) * edge * edge
+        for g in range(groups):
+            total = squares[g : g + 1, :]
+            for at in range(g * rows, (g + 1) * rows, LANES):
+                total += cross[:, at : at + LANES]
+            squares[g : g + 1, :] = total
+
     def send(here, mine, slots, peers, send_sem, recv_sem):
         for peer in peers:
             pltpu.make_async_remote_copy(
@@ -228,6 +340,18 @@
     def _(g):
         more = jnp.dot(edge_t[chunk(g), :], edge_op[:, LANES:], preferred_element_type=jnp.float32)
         second[chunk(g), :] = second[chunk(g), :] + more
+
+    @pl.when(jnp.logical_not(is_inner))
+    def _():
+        far_r.wait_recv()
+
+        @pl.loop(0, groups)
+        def _(g):
+            far = from_far[:, chunk(g)]
+            edge = spread(jnp.where(is_first, far, 0.0), jnp.where(is_last, far, 0.0))
+            more = jnp.dot(edge, edge_op[...], preferred_element_type=jnp.float32)
+            first[chunk(g), :] = first[chunk(g), :] + more[:, :LANES]
+            second[chunk(g), :] = second[chunk(g), :] + more[:, LANES:]
 
     collect(n_a, slots_a, a_send, a_recv)
     energy = jnp.sum(slots_a[...], axis=0)
@@ -236,12 +360,21 @@
     send(in_b, mine_b, slots_b, peers_b, b_send, b_recv)
     collect(n_b, slots_b, b_send, b_recv)
     energy_ref[...] = jnp.sum(slots_b[...], axis=0) * (1.0 / points)
+    halo_r.wait_send()
+    halo_l.wait_send()
+
+    @pl.when(jnp.logical_not(is_inner))
+    def _():
+        middle_r.wait_send()
 
 
 def store(first, second, energy_ref, first_hbm, second_hbm, out_ref, sems):
+    lines, pieces = first.shape[0], sems.shape[1]
+    step = lines // pieces
     outs = [
-        pltpu.make_async_copy(first, first_hbm, sems.at[0]),
-        pltpu.make_async_copy(second, second_hbm, sems.at[1]),
+        pltpu.make_async_copy(src.at[pl.ds(n * step, step)], dst.at[pl.ds(n * step, step)], sems.at[side, n])
+        for n in range(pieces)
+        for side, (src, dst) in enumerate(((first, first_hbm), (second, second_hbm)))
     ]
     for copy in outs:
         copy.start()
@@ -292,6 +425,10 @@
             pltpu.VMEM((4, lines), f32),
             pltpu.VMEM((4, lines), f32),
             pltpu.VMEM((4, lines), f32),
+            pltpu.VMEM((4, lines), f32),
+            pltpu.VMEM((4, lines + lanes), f32),
+            pltpu.VMEM((4, lines + lanes), f32),
+            pltpu.VMEM((2, 4, lines + lanes), f32),
             pltpu.VMEM((1, lanes), f32),
             pltpu.VMEM((n_a, 1, lanes), f32),
             pltpu.VMEM((1, lanes), f32),
@@ -299,6 +436,9 @@
             dma((groups,)),
             dma((4,)),
             dma((2,)),
+            dma((2,)),
+            dma,
+            dma,
             dma((2,)),
             dma, dma, dma, dma,
         ],
@@ -316,7 +456,7 @@
         out_shape=(whole, whole, jax.ShapeDtypeStruct((planes, comps), f32)),
         in_specs=[vmem] * 3,
         out_specs=(anywhere, anywhere, vmem),
-        scratch_shapes=[dma((2,))],
+        scratch_shapes=[dma((2, groups))],
     )(*(pltpu.with_memory_space_constraint(a, pltpu.VMEM) for a in (first, second, energy)))
     return (first.reshape(velocity.shape), second.reshape(velocity.shape), energy.T)
 

time: 33.5 us -> 32.3 us (0.964)
  Pallas kernels: 32.8 us -> 31.5 us
    pallas_call x1, Pallas kernels: 30.8 us -> 29.5 us  [on_device(): pl.pallas_call(functools.partial(kernel, places, groups, rows, points), o...]
where the time goes in v3:
time: 32.3 us; the launch traced here: 32.2 us
  Pallas kernels  31.5 us (98%)
  between operations  0.64 us (2%)
    pallas_call x1, Pallas kernels, on_device(): pl.pallas_call(functools.partial(kernel, places, groups, rows, points), o...  29.5 us
    pallas_call x1, Pallas kernels, on_device(): pl.pallas_call(store, out_shape=(whole, whole, jax.ShapeDtypeStruct((plan...  2.05 us

profile of v3, /device:TPU:1, one launch (start us, length us, event | category | flops | bytes accessed | tf_op | source)
XLA Modules:
  0.0 32.2 jit_solution(10668898164322887678)
XLA Ops:
  0.6 29.5 %shard_map.76 = (f32[2304,128]{1,0:T(8,128)S(1)}, f32[2304,128]{1,0:T(8,128)S(1)}, f32[1,128]{1,0:T(1,128)S(1)}) custom-call(f32[2304,128]{1,0:T(8,128)} %bitcast.7, f32[280,128]{1,0:T(8,128)} %constant.2.clone.const_hbm, s32[1,128]{1,0:T(1,128)} %bitcast.8, f32[1,64]{1,0:T(1,128)} %bitcast.9, f32[1,64]{1,0:T(1,128)} %bitcast.10), custom_call_target="tpu_custom_call" | custom-call | tf_op jit(solution)/shard_map/pallas_call | solution.py:404
  30.1 2.1 %shard_map.77 = (f32[2304,128]{1,0:T(8,128)}, f32[2304,128]{1,0:T(8,128)}, f32[2,3]{1,0:T(2,128)}) custom-call(f32[2304,128]{1,0:T(8,128)S(1)} %get-tuple-element.9.first, f32[2304,128]{1,0:T(8,128)S(1)} %get-tuple-element.10.second, f32[1,128]{1,0:T(1,128)S(1)} %get-tuple-element.11.energy_ref), custom_call_target="tpu_custom_call" | custom-call | tf_op jit(solution)/shard_map/pallas_call | solution.py:454

commit v4 on v3

--- a/solution.py
+++ b/solution.py
@@ -54,7 +54,7 @@
     x, const, index, jac_tab, bend_tab, split, edge_t, op, edge_op, squares,
     to_right, to_left, from_left, from_right, from_far, to_middle_r, to_middle_l, middle,
     mine_a, slots_a, mine_b, slots_b,
-    x_sem, in_sem, halo_send, halo_recv, far_recv, mid_send, mid_recv, a_send, a_recv, b_send, b_recv,
+    ready, x_sem, in_sem, halo_send, halo_recv, far_recv, mid_send, mid_recv, a_send, a_recv, b_send, b_recv,
 ):
     n_zh, n_y, n_core, n_zl, n_x = places
     n_gx = n_zh * n_y * n_core
@@ -62,36 +62,50 @@
     halves_x = n_x // 2
     n_a, n_b = n_y * 2, n_z * n_core * halves_x
     gx, gz = lax.axis_index("gx"), lax.axis_index("gz")
-    core = gx % n_core
-    y = (gx // n_core) % n_y
-    zh = gx // (n_core * n_y)
-    xx = gz % n_x
-    zl = gz // n_x
+    div, rem = lax.div, lax.rem
+    core = rem(gx, n_core)
+    y = rem(div(gx, n_core), n_y)
+    zh = div(gx, n_core * n_y)
+    xx = rem(gz, n_x)
+    zl = div(gz, n_x)
     z = zh * n_zl + zl
-    in_a = y * 2 + xx % 2
-    in_b = (z * n_core + core) * halves_x + xx // 2
+    x_low = rem(xx, 2)
+    in_a = y * 2 + x_low
+    in_b = (z * n_core + core) * halves_x + div(xx, 2)
 
     def turned(place, by, size):
         place = place + by
         return jnp.where(place >= size, place - size, place)
 
-    pair_a = xx + 1 - 2 * (xx % 2)
+    pair_a = xx + 1 - 2 * x_low
     ys = [(zh * n_y + turned(y, by, n_y)) * n_core + core for by in range(n_y)]
     peers_a = [
-        (min(by, n_y - by) + across, ys[by], zl * n_x + (pair_a if across else xx))
+        (min(by, n_y - by), across, {"gx": ys[by], "gz": zl * n_x + (pair_a if across else xx)})
         for by in range(n_y) for across in range(2) if by + across
     ]
     zs = [turned(z, by, n_z) for by in range(n_z)]
+    zs = [(div(there, n_zl) * n_y + y, rem(there, n_zl) * n_x) for there in zs]
     peers_b = [
         (
-            min(by, n_z - by) + across,
-            ((zs[by] // n_zl) * n_y + y) * n_core + (1 - core if other else core),
-            (zs[by] % n_zl) * n_x + (n_x - 1 - xx if across else xx),
+            min(by, n_z - by),
+            across + other,
+            {
+                "gx": zs[by][0] * n_core + (1 - core if other else core),
+                "gz": zs[by][1] + (n_x - 1 - xx if across else xx),
+            },
         )
         for by in range(n_z) for other in range(n_core) for across in range(halves_x) if by + other + across
     ]
-    peers_a = [{"gx": p[1], "gz": p[2]} for p in sorted(peers_a, key=lambda p: -p[0])]
-    peers_b = [{"gx": p[1], "gz": p[2]} for p in sorted(peers_b, key=lambda p: -p[0])]
+    peers_a.sort(key=lambda p: -p[0] - p[1])
+    peers_b.sort(key=lambda p: -p[0] - p[1])
+
+    near_y, near_z = max(n_y // 4, 1), max(n_z // 4, 1)
+    round_one = [p for p in peers_b if p[0] <= near_z] + [p for p in peers_a if p[0] <= near_y]
+    round_two = [p for p in peers_b if p[:2] == (near_z, 0) and n_z >= 4]
+    round_two += [p for p in peers_a if p[:2] == (near_y, 0) and n_y >= 4]
+    peers_a, peers_b, round_one, round_two = (
+        [p[2] for p in peers] for peers in (peers_a, peers_b, round_one, round_two)
+    )
 
     lines = groups * rows
     quarter = n_z // 4
@@ -101,13 +115,13 @@
     def in_z(by, at_last):
         there = turned(z, by % n_z, n_z)
         within = n_y * n_core - 1 if at_last else 0
-        return {"gx": (there // n_zl) * n_y * n_core + within, "gz": (there % n_zl) * n_x + xx}
+        return {"gx": div(there, n_zl) * n_y * n_core + within, "gz": rem(there, n_zl) * n_x + xx}
 
     ahead, behind = in_z(quarter, True), in_z(-quarter, True)
     ahead_first = in_z(quarter, False)
 
-    right = {"gx": (gx + 1) % n_gx, "gz": gz}
-    left = {"gx": (gx + n_gx - 1) % n_gx, "gz": gz}
+    right = {"gx": rem(gx + 1, n_gx), "gz": gz}
+    left = {"gx": rem(gx + n_gx - 1, n_gx), "gz": gz}
 
     def chunk(g):
         return pl.ds(pl.multiple_of(g * rows, rows), rows)
@@ -121,27 +135,37 @@
             ((const_hbm, const), (index_hbm, index), (jac_hbm, jac_tab), (bend_hbm, bend_tab))
         )
     ]
-    barrier = pltpu.get_barrier_semaphore()
-    pl.semaphore_signal(barrier, inc=1, device_id=right, device_id_type=MESH)
-    pl.semaphore_signal(barrier, inc=1, device_id=left, device_id_type=MESH)
     for copy in smalls:
         copy.start()
     for g in range(groups):
         load(g).start()
 
-    for peer in peers_a + peers_b:
-        pl.semaphore_signal(barrier, inc=1, device_id=peer, device_id_type=MESH)
+    barrier = pltpu.get_barrier_semaphore()
+
+    def greet(semaphore, peer):
+        pl.semaphore_signal(semaphore, inc=1, device_id=peer, device_id_type=MESH)
 
     @pl.when(is_last)
     def _():
-        for peer in (ahead, behind, ahead_first):
-            pl.semaphore_signal(barrier, inc=1, device_id=peer, device_id_type=MESH)
+        for peer in (ahead_first, ahead, behind):
+            greet(barrier, peer)
         from_right[...] = jnp.zeros_like(from_right)
 
     @pl.when(is_first)
     def _():
-        pl.semaphore_signal(barrier, inc=1, device_id=behind, device_id_type=MESH)
+        greet(barrier, behind)
         from_left[...] = jnp.zeros_like(from_left)
+
+    @pl.when(jnp.logical_not(is_last))
+    def _():
+        greet(barrier, right)
+
+    @pl.when(jnp.logical_not(is_first))
+    def _():
+        greet(barrier, left)
+
+    for peer in round_one:
+        greet(barrier, peer)
 
     for copy in smalls:
         copy.wait()
@@ -211,7 +235,7 @@
         to_middle_l[:, chunk(g)] = sums[12:16]
 
     pl.semaphore_wait(
-        barrier, 2 + (n_a - 1) + (n_b - 1) + jnp.where(is_last, 3, jnp.where(is_first, 1, 0))
+        barrier, len(round_one) + jnp.where(is_last, 4, 2)
     )
     middle_r = pltpu.make_async_remote_copy(
         to_middle_r, middle.at[0], mid_send, mid_recv.at[0], device_id=ahead, device_id_type=MESH
@@ -236,13 +260,12 @@
     def _():
         middle_r.start()
         halo_l.start()
-        far_r.start()
+        greet(ready, ahead_first)
 
     @pl.when(is_first)
     def _():
         middle_l.start()
         halo_r.start()
-        far_l.start()
 
     is_inner = jnp.logical_not(jnp.logical_or(is_last, is_first))
 
@@ -250,6 +273,9 @@
     def _():
         halo_r.start()
         halo_l.start()
+
+    for peer in round_two:
+        greet(ready, peer)
 
     op_high, op_low = halves(own_op)
     op[0:128, :] = op_high
@@ -267,6 +293,16 @@
         ) + jnp.dot(both, jnp.concatenate([low, low], axis=0), preferred_element_type=jnp.float32)
         first[chunk(g), :] = part[:, :LANES]
         second[chunk(g), :] = part[:, LANES:]
+
+    pl.semaphore_wait(ready, len(round_two) + jnp.where(is_first, 1, 0))
+
+    @pl.when(is_last)
+    def _():
+        far_r.start()
+
+    @pl.when(is_first)
+    def _():
+        far_l.start()
 
     @pl.when(jnp.logical_not(is_first))
     def _():
@@ -433,6 +469,7 @@
             pltpu.VMEM((n_a, 1, lanes), f32),
             pltpu.VMEM((1, lanes), f32),
             pltpu.VMEM((n_b, 1, lanes), f32),
+            pltpu.SemaphoreType.REGULAR,
             dma((groups,)),
             dma((4,)),
             dma((2,)),

time: 32.3 us -> 31.9 us (0.988)
  Pallas kernels: 31.5 us -> 31.1 us
    pallas_call x1, Pallas kernels: 29.5 us -> 29.1 us  [on_device(): pl.pallas_call(functools.partial(kernel, places, groups, rows, points), o...]
where the time goes in v4:
time: 31.9 us; the launch traced here: 31.8 us
  Pallas kernels  31.1 us (97%)
  between operations  0.64 us (2%)
    pallas_call x1, Pallas kernels, on_device(): pl.pallas_call(functools.partial(kernel, places, groups, rows, points), o...  29.1 us
    pallas_call x1, Pallas kernels, on_device(): pl.pallas_call(store, out_shape=(whole, whole, jax.ShapeDtypeStruct((plan...  2.05 us

profile of v4, /device:TPU:1, one launch (start us, length us, event | category | flops | bytes accessed | tf_op | source)
XLA Modules:
  0.0 31.8 jit_solution(11036662789806042848)
XLA Ops:
  0.6 29.1 %shard_map.76 = (f32[2304,128]{1,0:T(8,128)S(1)}, f32[2304,128]{1,0:T(8,128)S(1)}, f32[1,128]{1,0:T(1,128)S(1)}) custom-call(f32[2304,128]{1,0:T(8,128)} %bitcast.7, f32[280,128]{1,0:T(8,128)} %constant.2.clone.const_hbm, s32[1,128]{1,0:T(1,128)} %bitcast.8, f32[1,64]{1,0:T(1,128)} %bitcast.9, f32[1,64]{1,0:T(1,128)} %bitcast.10), custom_call_target="tpu_custom_call" | custom-call | tf_op jit(solution)/shard_map/pallas_call | solution.py:440
  29.7 2.1 %shard_map.77 = (f32[2304,128]{1,0:T(8,128)}, f32[2304,128]{1,0:T(8,128)}, f32[2,3]{1,0:T(2,128)}) custom-call(f32[2304,128]{1,0:T(8,128)S(1)} %get-tuple-element.9.first, f32[2304,128]{1,0:T(8,128)S(1)} %get-tuple-element.10.second, f32[1,128]{1,0:T(1,128)S(1)} %get-tuple-element.11.energy_ref), custom_call_target="tpu_custom_call" | custom-call | tf_op jit(solution)/shard_map/pallas_call | solution.py:491

commit v5 on v4

--- a/solution.py
+++ b/solution.py
@@ -363,11 +363,17 @@
         pltpu.make_async_copy(rest, rest, recv_sem).wait()
         pltpu.make_async_copy(rest, rest, send_sem).wait()
 
-    diagonal = lax.broadcasted_iota(jnp.int32, (8, LANES), 0) == lax.broadcasted_iota(
-        jnp.int32, (8, LANES), 1
-    )
+    planes, comps = energy_ref.shape
+    row = lax.broadcasted_iota(jnp.int32, (8, LANES), 0)
+    lane = lax.broadcasted_iota(jnp.int32, (8, LANES), 1)
     energy = jnp.sum(squares[...], axis=1, keepdims=True)
-    energy = jnp.sum(jnp.where(diagonal, energy, 0.0), axis=0, keepdims=True)
+    energy = jnp.concatenate(
+        [
+            jnp.sum(jnp.where(row == lane * planes + plane, energy, 0.0), axis=0, keepdims=True)
+            for plane in range(planes)
+        ],
+        axis=0,
+    )
     mine_a[...] = energy
     slots_a[in_a] = energy
     send(in_a, mine_a, slots_a, peers_a, a_send, a_recv)
@@ -395,7 +401,7 @@
     slots_b[in_b] = energy
     send(in_b, mine_b, slots_b, peers_b, b_send, b_recv)
     collect(n_b, slots_b, b_send, b_recv)
-    energy_ref[...] = jnp.sum(slots_b[...], axis=0) * (1.0 / points)
+    energy_ref[...] = jnp.sum(slots_b[...], axis=0)[:, :comps] * (1.0 / points)
     halo_r.wait_send()
     halo_l.wait_send()
 
@@ -404,22 +410,11 @@
         middle_r.wait_send()
 
 
-def store(first, second, energy_ref, first_hbm, second_hbm, out_ref, sems):
-    lines, pieces = first.shape[0], sems.shape[1]
-    step = lines // pieces
-    outs = [
-        pltpu.make_async_copy(src.at[pl.ds(n * step, step)], dst.at[pl.ds(n * step, step)], sems.at[side, n])
-        for n in range(pieces)
-        for side, (src, dst) in enumerate(((first, first_hbm), (second, second_hbm)))
-    ]
+def store(first, second, energy, first_hbm, second_hbm, energy_hbm, sems):
+    pairs = ((first, first_hbm), (second, second_hbm), (energy, energy_hbm))
+    outs = [pltpu.make_async_copy(src, dst, sems.at[n]) for n, (src, dst) in enumerate(pairs)]
     for copy in outs:
         copy.start()
-    planes, comps = out_ref.shape
-    energy = energy_ref[...]
-    for row in range(planes):
-        for col in range(comps):
-            at = col * planes + row
-            out_ref[row : row + 1, col : col + 1] = energy[:, at : at + 1]
     for copy in outs:
         copy.wait()
 
@@ -442,7 +437,7 @@
         out_shape=(
             pltpu.VMEM((lines, lanes), f32),
             pltpu.VMEM((lines, lanes), f32),
-            pltpu.VMEM((1, lanes), f32),
+            pltpu.VMEM((planes, comps), f32),
         ),
         in_specs=[anywhere] * 5,
         out_specs=(vmem, vmem, vmem),
@@ -465,10 +460,10 @@
             pltpu.VMEM((4, lines + lanes), f32),
             pltpu.VMEM((4, lines + lanes), f32),
             pltpu.VMEM((2, 4, lines + lanes), f32),
-            pltpu.VMEM((1, lanes), f32),
-            pltpu.VMEM((n_a, 1, lanes), f32),
-            pltpu.VMEM((1, lanes), f32),
-            pltpu.VMEM((n_b, 1, lanes), f32),
+            pltpu.VMEM((planes, lanes), f32),
+            pltpu.VMEM((n_a, planes, lanes), f32),
+            pltpu.VMEM((planes, lanes), f32),
+            pltpu.VMEM((n_b, planes, lanes), f32),
             pltpu.SemaphoreType.REGULAR,
             dma((groups,)),
             dma((4,)),
@@ -492,8 +487,8 @@
         store,
         out_shape=(whole, whole, jax.ShapeDtypeStruct((planes, comps), f32)),
         in_specs=[vmem] * 3,
-        out_specs=(anywhere, anywhere, vmem),
-        scratch_shapes=[dma((2, groups))],
+        out_specs=(anywhere, anywhere, anywhere),
+        scratch_shapes=[dma((3,))],
     )(*(pltpu.with_memory_space_constraint(a, pltpu.VMEM) for a in (first, second, energy)))
     return (first.reshape(velocity.shape), second.reshape(velocity.shape), energy.T)
 

time: 31.9 us -> 31.7 us (level)
    pallas_call x1, Pallas kernels: 2.05 us -> 1.43 us  [on_device(): pl.pallas_call(store, out_shape=(whole, whole, jax.ShapeDtypeStruct((plan...]
    pallas_call x1, Pallas kernels: 29.1 us -> 29.5 us  [on_device(): pl.pallas_call(functools.partial(kernel, places, groups, rows, points), o...]
where the time goes in v5:
time: 31.7 us; the launch traced here: 31.5 us
  Pallas kernels  30.9 us (97%)
  between operations  0.64 us (2%)
    pallas_call x1, Pallas kernels, on_device(): pl.pallas_call(functools.partial(kernel, places, groups, rows, points), o...  29.5 us
    pallas_call x1, Pallas kernels, on_device(): pl.pallas_call(store, out_shape=(whole, whole, jax.ShapeDtypeStruct((plan...  1.43 us

profile of v5, /device:TPU:1, one launch (start us, length us, event | category | flops | bytes accessed | tf_op | source)
XLA Modules:
  0.0 31.5 jit_solution(5978955311064659163)
XLA Ops:
  0.6 29.5 %shard_map.76 = (f32[2304,128]{1,0:T(8,128)S(1)}, f32[2304,128]{1,0:T(8,128)S(1)}, f32[2,3]{1,0:T(2,128)S(1)}) custom-call(f32[2304,128]{1,0:T(8,128)} %bitcast.7, f32[280,128]{1,0:T(8,128)} %constant.2.clone.const_hbm, s32[1,128]{1,0:T(1,128)} %bitcast.8, f32[1,64]{1,0:T(1,128)} %bitcast.9, f32[1,64]{1,0:T(1,128)} %bitcast.10), custom_call_target="tpu_custom_call" | custom-call | tf_op jit(solution)/shard_map/pallas_call | solution.py:435
  30.1 1.4 %shard_map.77 = (f32[2304,128]{1,0:T(8,128)}, f32[2304,128]{1,0:T(8,128)}, f32[2,3]{1,0:T(2,128)}) custom-call(f32[2304,128]{1,0:T(8,128)S(1)} %get-tuple-element.9.first, f32[2304,128]{1,0:T(8,128)S(1)} %get-tuple-element.10.second, f32[2,3]{1,0:T(2,128)S(1)} %get-tuple-element.11.energy), custom_call_target="tpu_custom_call" | custom-call | tf_op jit(solution)/shard_map/pallas_call | solution.py:486

commit v6 on v5

--- a/solution.py
+++ b/solution.py
@@ -132,7 +132,9 @@
     smalls = [
         pltpu.make_async_copy(src, dst, in_sem.at[n])
         for n, (src, dst) in enumerate(
-            ((const_hbm, const), (index_hbm, index), (jac_hbm, jac_tab), (bend_hbm, bend_tab))
+            (
+                (const_hbm, const), (index_hbm, index.at[0]), (jac_hbm, jac_tab.at[0]), (bend_hbm, bend_tab.at[0])
+            )
         )
     ]
     for copy in smalls:
@@ -156,25 +158,25 @@
         greet(barrier, behind)
         from_left[...] = jnp.zeros_like(from_left)
 
-    @pl.when(jnp.logical_not(is_last))
-    def _():
-        greet(barrier, right)
-
-    @pl.when(jnp.logical_not(is_first))
-    def _():
-        greet(barrier, left)
-
     for peer in round_one:
         greet(barrier, peer)
 
+    @pl.when(jnp.logical_not(is_last))
+    def _():
+        greet(barrier, right)
+
+    @pl.when(jnp.logical_not(is_first))
+    def _():
+        greet(barrier, left)
+
     for copy in smalls:
         copy.wait()
-    table_rows = jac_tab.shape[1]
+    table_rows = jac_tab.shape[2]
     onehot = (
-        lax.broadcasted_iota(jnp.int32, (table_rows, LANES), 0) == index[...]
+        lax.broadcasted_iota(jnp.int32, (table_rows, LANES), 0) == index[0]
     ).astype(jnp.float32)
     tables = jnp.concatenate(
-        [jnp.broadcast_to(jac_tab[...], (8, table_rows)), jnp.broadcast_to(bend_tab[...], (8, table_rows))],
+        [jnp.broadcast_to(jac_tab[0], (8, table_rows)), jnp.broadcast_to(bend_tab[0], (8, table_rows))],
         axis=0,
     )
     metric = jnp.dot(tables, onehot, precision=lax.Precision.HIGHEST)
@@ -198,8 +200,8 @@
             ((sums_of * sums_of, 1.0), (sums_of * edge_of, 2.0), (edge_of * edge_of, 1.0))
         ):
             total = jnp.sum(product, axis=1, keepdims=True) * times
-            ref[row : row + 1, lines:] = jnp.broadcast_to(total, (1, LANES))
-        ref[3:4, lines:] = jnp.zeros((1, LANES), jnp.float32)
+            ref[row : row + 1, lines : lines + LANES] = jnp.broadcast_to(total, (1, LANES))
+        ref[3:4, lines : lines + LANES] = jnp.zeros((1, LANES), jnp.float32)
     out_rows = const[272:280, :]
     leave_high, leave_low = halves(
         jnp.concatenate(
@@ -237,23 +239,24 @@
     pl.semaphore_wait(
         barrier, len(round_one) + jnp.where(is_last, 4, 2)
     )
+    full, fuller = pl.ds(0, lines), pl.ds(0, lines + LANES)
     middle_r = pltpu.make_async_remote_copy(
-        to_middle_r, middle.at[0], mid_send, mid_recv.at[0], device_id=ahead, device_id_type=MESH
+        to_middle_r.at[:, fuller], middle.at[0, :, fuller], mid_send, mid_recv.at[0], device_id=ahead, device_id_type=MESH
     )
     middle_l = pltpu.make_async_remote_copy(
-        to_middle_l, middle.at[1], mid_send, mid_recv.at[1], device_id=behind, device_id_type=MESH
+        to_middle_l.at[:, fuller], middle.at[1, :, fuller], mid_send, mid_recv.at[1], device_id=behind, device_id_type=MESH
     )
     halo_r = pltpu.make_async_remote_copy(
-        to_right, from_left, halo_send.at[0], halo_recv.at[0], device_id=right, device_id_type=MESH
+        to_right.at[:, full], from_left.at[:, full], halo_send.at[0], halo_recv.at[0], device_id=right, device_id_type=MESH
     )
     halo_l = pltpu.make_async_remote_copy(
-        to_left, from_right, halo_send.at[1], halo_recv.at[1], device_id=left, device_id_type=MESH
+        to_left.at[:, full], from_right.at[:, full], halo_send.at[1], halo_recv.at[1], device_id=left, device_id_type=MESH
     )
     far_r = pltpu.make_async_remote_copy(
-        to_right, from_far, halo_send.at[0], far_recv, device_id=right, device_id_type=MESH
+        to_right.at[:, full], from_far.at[:, full], halo_send.at[0], far_recv, device_id=right, device_id_type=MESH
     )
     far_l = pltpu.make_async_remote_copy(
-        to_left, from_far, halo_send.at[1], far_recv, device_id=left, device_id_type=MESH
+        to_left.at[:, full], from_far.at[:, full], halo_send.at[1], far_recv, device_id=left, device_id_type=MESH
     )
 
     @pl.when(is_last)
@@ -338,7 +341,7 @@
         left_sum, left_edge = middle[1, 0:1, whole], middle[1, 1:2, whole]
 
         def again(side, row):
-            return jnp.concatenate([middle[side, row : row + 1, lines:]] * (lines // LANES), axis=1)
+            return jnp.concatenate([middle[side, row : row + 1, lines : lines + LANES]] * (lines // LANES), axis=1)
 
         cross = 2.0 * (
             right_sum * middle[1, 2:3, whole] + right_edge * middle[1, 3:4, whole]
@@ -355,7 +358,7 @@
     def send(here, mine, slots, peers, send_sem, recv_sem):
         for peer in peers:
             pltpu.make_async_remote_copy(
-                mine, slots.at[here], send_sem, recv_sem, device_id=peer, device_id_type=MESH
+                mine.at[0], slots.at[here], send_sem, recv_sem, device_id=peer, device_id_type=MESH
             ).start()
 
     def collect(n, slots, send_sem, recv_sem):
@@ -374,7 +377,7 @@
         ],
         axis=0,
     )
-    mine_a[...] = energy
+    mine_a[0] = energy
     slots_a[in_a] = energy
     send(in_a, mine_a, slots_a, peers_a, a_send, a_recv)
 
@@ -383,6 +386,11 @@
         more = jnp.dot(edge_t[chunk(g), :], edge_op[:, LANES:], preferred_element_type=jnp.float32)
         second[chunk(g), :] = second[chunk(g), :] + more
 
+    collect(n_a, slots_a, a_send, a_recv)
+    energy = jnp.sum(slots_a[0:n_a], axis=0)
+    mine_b[0] = energy
+    slots_b[in_b] = energy
+    send(in_b, mine_b, slots_b, peers_b, b_send, b_recv)
     @pl.when(jnp.logical_not(is_inner))
     def _():
         far_r.wait_recv()
@@ -395,13 +403,8 @@
             first[chunk(g), :] = first[chunk(g), :] + more[:, :LANES]
             second[chunk(g), :] = second[chunk(g), :] + more[:, LANES:]
 
-    collect(n_a, slots_a, a_send, a_recv)
-    energy = jnp.sum(slots_a[...], axis=0)
-    mine_b[...] = energy
-    slots_b[in_b] = energy
-    send(in_b, mine_b, slots_b, peers_b, b_send, b_recv)
     collect(n_b, slots_b, b_send, b_recv)
-    energy_ref[...] = jnp.sum(slots_b[...], axis=0)[:, :comps] * (1.0 / points)
+    energy_ref[...] = jnp.sum(slots_b[0:n_b], axis=0)[:, :comps] * (1.0 / points)
     halo_r.wait_send()
     halo_l.wait_send()
 
@@ -444,26 +447,26 @@
         scratch_shapes=[
             pltpu.VMEM((lines, lanes), f32),
             pltpu.VMEM(const.shape, f32),
-            pltpu.VMEM((1, lanes), jnp.int32),
-            pltpu.VMEM((1, table_rows), f32),
-            pltpu.VMEM((1, table_rows), f32),
+            pltpu.VMEM((8, 1, lanes), jnp.int32),
+            pltpu.VMEM((8, 1, table_rows), f32),
+            pltpu.VMEM((8, 1, table_rows), f32),
             pltpu.VMEM((lines, 2 * lanes), bf16),
             pltpu.VMEM((lines, 32), bf16),
             pltpu.VMEM((2 * lanes, 2 * lanes), bf16),
             pltpu.VMEM((32, 2 * lanes), bf16),
             pltpu.VMEM((8, lanes), f32),
-            pltpu.VMEM((4, lines), f32),
-            pltpu.VMEM((4, lines), f32),
-            pltpu.VMEM((4, lines), f32),
-            pltpu.VMEM((4, lines), f32),
-            pltpu.VMEM((4, lines), f32),
             pltpu.VMEM((4, lines + lanes), f32),
             pltpu.VMEM((4, lines + lanes), f32),
-            pltpu.VMEM((2, 4, lines + lanes), f32),
-            pltpu.VMEM((planes, lanes), f32),
-            pltpu.VMEM((n_a, planes, lanes), f32),
-            pltpu.VMEM((planes, lanes), f32),
-            pltpu.VMEM((n_b, planes, lanes), f32),
+            pltpu.VMEM((4, lines + lanes), f32),
+            pltpu.VMEM((4, lines + lanes), f32),
+            pltpu.VMEM((4, lines + lanes), f32),
+            pltpu.VMEM((4, lines + 2 * lanes), f32),
+            pltpu.VMEM((4, lines + 2 * lanes), f32),
+            pltpu.VMEM((2, 4, lines + 2 * lanes), f32),
+            pltpu.VMEM((8, planes, lanes), f32),
+            pltpu.VMEM((n_a + 8, planes, lanes), f32),
+            pltpu.VMEM((8, planes, lanes), f32),
+            pltpu.VMEM((n_b + 8, planes, lanes), f32),
             pltpu.SemaphoreType.REGULAR,
             dma((groups,)),
             dma((4,)),

time: 31.7 us -> 31.7 us (level)
  no operation moved by 1% of the time
where the time goes in v6:
time: 31.7 us; the launch traced here: 31.5 us
  Pallas kernels  30.9 us (97%)
  between operations  0.64 us (2%)
    pallas_call x1, Pallas kernels, on_device(): pl.pallas_call(functools.partial(kernel, places, groups, rows, points), o...  29.5 us
    pallas_call x1, Pallas kernels, on_device(): pl.pallas_call(store, out_shape=(whole, whole, jax.ShapeDtypeStruct((plan...  1.43 us

profile of v6, /device:TPU:1, one launch (start us, length us, event | category | flops | bytes accessed | tf_op | source)
XLA Modules:
  0.0 31.5 jit_solution(7137633469857970915)
XLA Ops:
  0.6 29.5 %shard_map.76 = (f32[2304,128]{1,0:T(8,128)S(1)}, f32[2304,128]{1,0:T(8,128)S(1)}, f32[2,3]{1,0:T(2,128)S(1)}) custom-call(f32[2304,128]{1,0:T(8,128)} %bitcast.7, f32[280,128]{1,0:T(8,128)} %constant.2.clone.const_hbm, s32[1,128]{1,0:T(1,128)} %bitcast.8, f32[1,64]{1,0:T(1,128)} %bitcast.9, f32[1,64]{1,0:T(1,128)} %bitcast.10), custom_call_target="tpu_custom_call" | custom-call | tf_op jit(solution)/shard_map/pallas_call | solution.py:438
  30.1 1.4 %shard_map.77 = (f32[2304,128]{1,0:T(8,128)}, f32[2304,128]{1,0:T(8,128)}, f32[2,3]{1,0:T(2,128)}) custom-call(f32[2304,128]{1,0:T(8,128)S(1)} %get-tuple-element.9.first, f32[2304,128]{1,0:T(8,128)S(1)} %get-tuple-element.10.second, f32[2,3]{1,0:T(2,128)S(1)} %get-tuple-element.11.energy), custom_call_target="tpu_custom_call" | custom-call | tf_op jit(solution)/shard_map/pallas_call | solution.py:489

commit v7 on v6

--- a/solution.py
+++ b/solution.py
@@ -361,10 +361,9 @@
                 mine.at[0], slots.at[here], send_sem, recv_sem, device_id=peer, device_id_type=MESH
             ).start()
 
-    def collect(n, slots, send_sem, recv_sem):
+    def collect(n, slots, semaphore):
         rest = slots.at[pl.ds(0, n - 1)]
-        pltpu.make_async_copy(rest, rest, recv_sem).wait()
-        pltpu.make_async_copy(rest, rest, send_sem).wait()
+        pltpu.make_async_copy(rest, rest, semaphore).wait()
 
     planes, comps = energy_ref.shape
     row = lax.broadcasted_iota(jnp.int32, (8, LANES), 0)
@@ -386,7 +385,7 @@
         more = jnp.dot(edge_t[chunk(g), :], edge_op[:, LANES:], preferred_element_type=jnp.float32)
         second[chunk(g), :] = second[chunk(g), :] + more
 
-    collect(n_a, slots_a, a_send, a_recv)
+    collect(n_a, slots_a, a_recv)
     energy = jnp.sum(slots_a[0:n_a], axis=0)
     mine_b[0] = energy
     slots_b[in_b] = energy
@@ -403,8 +402,10 @@
             first[chunk(g), :] = first[chunk(g), :] + more[:, :LANES]
             second[chunk(g), :] = second[chunk(g), :] + more[:, LANES:]
 
-    collect(n_b, slots_b, b_send, b_recv)
+    collect(n_b, slots_b, b_recv)
     energy_ref[...] = jnp.sum(slots_b[0:n_b], axis=0)[:, :comps] * (1.0 / points)
+    collect(n_a, slots_a, a_send)
+    collect(n_b, slots_b, b_send)
     halo_r.wait_send()
     halo_l.wait_send()
 

time: 31.7 us -> 31.7 us (level)
  no operation moved by 1% of the time
where the time goes in v7:
time: 31.7 us; the launch traced here: 31.5 us
  Pallas kernels  30.9 us (97%)
  between operations  0.64 us (2%)
    pallas_call x1, Pallas kernels, on_device(): pl.pallas_call(functools.partial(kernel, places, groups, rows, points), o...  29.5 us
    pallas_call x1, Pallas kernels, on_device(): pl.pallas_call(store, out_shape=(whole, whole, jax.ShapeDtypeStruct((plan...  1.43 us

profile of v7, /device:TPU:1, one launch (start us, length us, event | category | flops | bytes accessed | tf_op | source)
XLA Modules:
  0.0 31.5 jit_solution(2711223720280569437)
XLA Ops:
  0.6 29.5 %shard_map.76 = (f32[2304,128]{1,0:T(8,128)S(1)}, f32[2304,128]{1,0:T(8,128)S(1)}, f32[2,3]{1,0:T(2,128)S(1)}) custom-call(f32[2304,128]{1,0:T(8,128)} %bitcast.7, f32[280,128]{1,0:T(8,128)} %constant.2.clone.const_hbm, s32[1,128]{1,0:T(1,128)} %bitcast.8, f32[1,64]{1,0:T(1,128)} %bitcast.9, f32[1,64]{1,0:T(1,128)} %bitcast.10), custom_call_target="tpu_custom_call" | custom-call | tf_op jit(solution)/shard_map/pallas_call | solution.py:439
  30.1 1.4 %shard_map.77 = (f32[2304,128]{1,0:T(8,128)}, f32[2304,128]{1,0:T(8,128)}, f32[2,3]{1,0:T(2,128)}) custom-call(f32[2304,128]{1,0:T(8,128)S(1)} %get-tuple-element.9.first, f32[2304,128]{1,0:T(8,128)S(1)} %get-tuple-element.10.second, f32[2,3]{1,0:T(2,128)S(1)} %get-tuple-element.11.energy), custom_call_target="tpu_custom_call" | custom-call | tf_op jit(solution)/shard_map/pallas_call | solution.py:490
